TPU v7x, 32 devices: a whole 2x2x4 slice. The times are simulated.
32 devices in a mesh: seq: 8 (over y, x, core), chan: 4 (over z).
Axes of the slice: x: 2, y: 2, z: 4, core: 2. Of those that a mesh axis runs over, the one named last changes fastest.
Arguments:
- hidden_states: bfloat16 [4096, 2048], P('chan', 'seq'), may hold values from -700 to 700
- norm_gain: float32 [4096], P('chan'), may hold values from 0.1 to 1.9
- short_filter: float32 [4096, 128], P('chan'), may hold values from -0.5 to 0.5
- long_filter: bfloat16 [4096, 2048], P('chan', 'seq'), may hold values from -0.125 to 0.125
- long_bias: float32 [4096], P('chan'), may hold values from -4 to 4
- gate_stream: bfloat16 [4096, 2048], P('chan', 'seq'), may hold values from -6 to 6
- upstream: bfloat16 [4096, 2048], P(None, 'seq'), may hold values from -6 to 6
Outputs:
- mixed: bfloat16 [4096, 2048], P('chan', 'seq')
- weight_grad: float32 [4096, 4096], P('seq', 'chan')
All inputs are finite; a program needn't handle non-finite values.
Results may differ from a plain program's by a relative error of at most 0.015.
Values may be sent and summed in bfloat16 or wider, within the bound.
A program may use at most 64 MiB of HBM per device.

v0:
```python
import math
import jax
import jax.numpy as jnp
from jax import lax
from jax.sharding import PartitionSpec as P

D = 4096
EPSILON = 1e-05


def passed_along(value, axis, by):
    devices = lax.axis_size(axis)
    pairs = [(i, i + by) for i in range(devices) if 0 <= i + by < devices]
    return lax.ppermute(value, axis, pairs)


def short_conv(padded, taps):
    kernel = taps[:, ::-1][:, None, :]
    result = lax.conv_general_dilated(
        padded[None],
        kernel,
        (1,),
        "VALID",
        dimension_numbers=("NCH", "OIH", "NCH"),
        feature_group_count=padded.shape[0],
        precision=lax.Precision.HIGHEST,
    )
    return result[0]


def twiddle(row_total, col_total, modulus, direction):
    product = (
        jnp.arange(row_total, dtype=jnp.int32)[:, None]
        * jnp.arange(col_total, dtype=jnp.int32)[None, :]
        % modulus
    )
    angles = direction * 2.0 * math.pi * product.astype(jnp.float32) / modulus
    return (jnp.cos(angles), jnp.sin(angles))


def product_einsum(form, left, right):
    return jnp.einsum(form, left, right, precision=lax.Precision.HIGHEST)


def split_table(table):
    upper = table.astype(jnp.bfloat16)
    lower = (table - upper.astype(jnp.float32)).astype(jnp.bfloat16)
    return (upper, lower)


def table_product(table, grid):
    upper, lower = split_table(table)
    first = jnp.einsum("kn,cnm->ckm", upper, grid, preferred_element_type=jnp.float32)
    return first + jnp.einsum("kn,cnm->ckm", lower, grid, preferred_element_type=jnp.float32)


def forward_real(signal, factor_a, factor_b):
    length = factor_a * factor_b
    seq_total = signal.shape[1]
    kept_in = -(-seq_total // factor_b)
    filled = jnp.pad(signal, ((0, 0), (0, kept_in * factor_b - seq_total)))
    grid = filled.reshape(signal.shape[0], kept_in, factor_b)
    outer_re, outer_im = twiddle(factor_a, kept_in, factor_a, -1.0)
    section_re = table_product(outer_re, grid)
    section_im = table_product(outer_im, grid)
    turn_re, turn_im = twiddle(factor_a, factor_b, length, -1.0)
    rotated_re = section_re * turn_re - section_im * turn_im
    rotated_im = section_re * turn_im + section_im * turn_re
    inner_re, inner_im = twiddle(factor_b, factor_b, factor_b, -1.0)
    result_re = product_einsum("ckm,jm->ckj", rotated_re, inner_re) - product_einsum(
        "ckm,jm->ckj", rotated_im, inner_im
    )
    result_im = product_einsum("ckm,jm->ckj", rotated_re, inner_im) + product_einsum(
        "ckm,jm->ckj", rotated_im, inner_re
    )
    return (result_re, result_im)


def inverse_real(spec_re, spec_im, factor_a, factor_b, kept_rows):
    length = factor_a * factor_b
    inner_re, inner_im = twiddle(factor_b, factor_b, factor_b, 1.0)
    section_re = product_einsum("ckj,mj->ckm", spec_re, inner_re) - product_einsum(
        "ckj,mj->ckm", spec_im, inner_im
    )
    section_im = product_einsum("ckj,mj->ckm", spec_re, inner_im) + product_einsum(
        "ckj,mj->ckm", spec_im, inner_re
    )
    turn_re, turn_im = twiddle(factor_a, factor_b, length, 1.0)
    rotated_re = section_re * turn_re - section_im * turn_im
    rotated_im = section_re * turn_im + section_im * turn_re
    outer_re, outer_im = twiddle(kept_rows, factor_a, factor_a, 1.0)
    result = product_einsum("nk,ckm->cnm", outer_re, rotated_re) - product_einsum(
        "nk,ckm->cnm", outer_im, rotated_im
    )
    return result.reshape(result.shape[0], kept_rows * factor_b) / length


def long_convolution(signal, filt):
    seq_total = signal.shape[1]
    length = 2 * seq_total
    factor_a = 1
    for divisor in range(1, math.isqrt(length) + 1):
        if length % divisor == 0:
            factor_a = divisor
    factor_b = length // factor_a
    signal_re, signal_im = forward_real(signal, factor_a, factor_b)
    filter_re, filter_im = forward_real(filt, factor_a, factor_b)
    joint_re = signal_re * filter_re - signal_im * filter_im
    joint_im = signal_re * filter_im + signal_im * filter_re
    kept_rows = -(-seq_total // factor_b)
    return inverse_real(joint_re, joint_im, factor_a, factor_b, kept_rows)[:, :seq_total]


def shards(hidden_states, norm_gain, short_filter, long_filter, long_bias, gate_stream, upstream):
    states = hidden_states.astype(jnp.float32)
    partial_squares = jnp.sum(states * states, axis=0)
    squares = lax.psum(partial_squares, "chan")
    normed = (states * lax.rsqrt(squares / D + EPSILON)[None, :] * norm_gain[:, None]).astype(
        jnp.bfloat16
    )
    tap_count = short_filter.shape[1]
    width_local = hidden_states.shape[0] // lax.axis_size("seq")
    owner_index = lax.axis_index("seq")
    bias_slice = lax.dynamic_slice_in_dim(long_bias, owner_index * width_local, width_local)
    tail_cols = normed[:, normed.shape[1] - tap_count :]
    from_left = passed_along(tail_cols, "seq", 1)
    padded = jnp.concatenate(
        [from_left[:, 1:].astype(jnp.float32), normed.astype(jnp.float32)], axis=1
    )
    short_out = short_conv(padded, short_filter).astype(jnp.bfloat16)
    short_whole, filter_whole = (
        lax.all_to_all(short_out, "seq", split_axis=0, concat_axis=1, tiled=True),
        lax.all_to_all(long_filter, "seq", split_axis=0, concat_axis=1, tiled=True),
    )
    long_conv = long_convolution(short_whole, filter_whole)
    long_whole = (long_conv + bias_slice[:, None] * short_whole.astype(jnp.float32)).astype(
        jnp.bfloat16
    )
    long_out = lax.all_to_all(long_whole, "seq", split_axis=1, concat_axis=0, tiled=True)
    mixed = (gate_stream.astype(jnp.float32) * long_out.astype(jnp.float32)).astype(jnp.bfloat16)
    mixed_whole = lax.all_gather(mixed, "seq", axis=1, tiled=True)
    owned = lax.all_to_all(upstream, "seq", split_axis=0, concat_axis=1, tiled=True)
    weight_grad = lax.dot_general(
        owned, mixed_whole, (((1,), (1,)), ((), ())), preferred_element_type=jnp.float32
    )
    return (mixed, weight_grad)


def solution(mesh):
    placed = (
        P("chan", "seq"),
        P("chan"),
        P("chan", None),
        P("chan", "seq"),
        P("chan"),
        P("chan", "seq"),
        P(None, "seq"),
    )
    return jax.shard_map(
        shards,
        mesh=mesh,
        in_specs=placed,
        out_specs=(P("chan", "seq"), P("seq", "chan")),
        check_vma=False,
    )
```

profile of v0, /device:TPU:0, one launch (start us, length us, event | category | flops | bytes accessed | tf_op | source)
XLA Modules:
  0.0 184.4 jit_solution(16678184828693716588)
XLA Ops:
  7.2 1.3 fusion.43
  8.4 13.5 %psum.7 = f32[256]{0:T(256)S(1)} all-reduce(f32[256]{0:T(256)S(1)} %fusion.43), channel_id=1, replica_groups=mesh['seq'=8,'chan'=4] {'chan'}, use_global_device_ids=true, to_apply=%region_1.0 | all-reduce | flops 256 | bytes 2048 | tf_op jit(solution)/shard_map/psum | solution.py:117
  21.9 1.2 fusion.45
  23.2 1.3 collective-permute-start
  24.5 4.6 %all-to-all-start.1 = ((bf16[8,128,256]{2,1,0:T(8,128)(2,1)}), bf16[8,128,256]{2,1,0:T(8,128)(2,1)S(1)}, u32[]{:S(2)}, u32[]{:S(2)}) async-start(bf16[8,128,256]{2,1,0:T(8,128)(2,1)} %bitcast.13), calls=%async_computation.1 | async-start | bytes 1048576 | tf_op jit(solution)/shard_map/all_to_all | solution.py:133
  30.0 1.0 copy.57
  32.8 2.2 %copy.56 = bf16[1,1024,383]{1,0,2:T(2,128)(2,1)S(1)} copy(bf16[1,1024,383]{2,1,0:T(8,128)(2,1)S(1)} %maximum_bitcast_fusion) | data formatting | bytes 1568768 | tf_op jit(solution)/shard_map/broadcast_in_dim | solution.py:20
  35.1 12.7 %convolution_convert_fusion = bf16[1,1024,256]{1,0,2:T(2,128)(2,1)S(1)} fusion(bf16[1,1024,383]{1,0,2:T(2,128)(2,1)S(1)} %copy.56, f32[1024,1,128]{0,1,2:T(1,128)} %copy.57), kind=kOutput, calls=%fused_computation.43 | convolution fusion | flops 402915328 | bytes 1832960 | tf_op jit(solution)/shard_map/conv_general_dilated | solution.py:19
  47.8 2.0 %copy.58 = bf16[1,1024,256]{2,1,0:T(8,128)(2,1)} copy(bf16[1,1024,256]{1,0,2:T(2,128)(2,1)S(1)} %convolution_convert_fusion) | data formatting | bytes 1048576 | tf_op jit(solution)/shard_map/convert_element_type | solution.py:130
  49.8 4.2 %all-to-all-start = ((bf16[8,128,256]{2,1,0:T(8,128)(2,1)}), bf16[8,128,256]{2,1,0:T(8,128)(2,1)S(1)}, u32[]{:S(2)}, u32[]{:S(2)}) async-start(bf16[8,128,256]{2,1,0:T(8,128)(2,1)} %bitcast.2), calls=%async_computation | async-start | bytes 1048576 | tf_op jit(solution)/shard_map/all_to_all | solution.py:132
  56.2 1.6 subtract_bitcast_fusion
  57.8 3.3 %fusion.6 = f32[128,64,64]{0,2,1:T(8,128)S(1)} fusion(f32[128,64,64]{0,1,2:T(8,128)S(1)} %get-tuple-element.13), kind=kOutput, calls=%fused_computation.16 | convolution fusion | flops 402710528 | bytes 4194304 | tf_op jit(solution)/shard_map/ckm,jm->ckj/dot_general | solution.py:42
  61.2 3.4 %fusion.31 = f32[128,64,64]{0,2,1:T(8,128)S(1)} fusion(f32[128,64,64]{0,2,1:T(8,128)S(1)} %fusion.6, f32[128,64,64]{0,1,2:T(8,128)S(1)} %get-tuple-element.12), kind=kOutput, calls=%fused_computation.35 | convolution fusion | flops 403234816 | bytes 6291456 | tf_op jit(solution)/shard_map/ckm,jm->ckj/dot_general | solution.py:42
  64.6 3.6 %fusion.8 = f32[128,64,64]{0,2,1:T(8,128)S(1)} fusion(f32[128,64,64]{0,1,2:T(8,128)S(1)} %get-tuple-element.13), kind=kOutput, calls=%fused_computation.18 | convolution fusion | flops 402710528 | bytes 4194304 | tf_op jit(solution)/shard_map/ckm,jm->ckj/dot_general | solution.py:42
  68.1 4.7 %fusion.28 = f32[128,64,64]{0,2,1:T(8,128)} fusion(f32[128,64,64]{0,2,1:T(8,128)S(1)} %fusion.8, f32[128,64,64]{0,1,2:T(8,128)S(1)} %get-tuple-element.12), kind=kOutput, calls=%fused_computation.34 | convolution fusion | flops 403234816 | bytes 6291456 | tf_op jit(solution)/shard_map/ckm,jm->ckj/dot_general | solution.py:42
  74.9 1.6 fusion
  76.5 3.3 %fusion.16 = f32[128,64,64]{0,2,1:T(8,128)S(1)} fusion(f32[128,64,64]{0,1,2:T(8,128)S(1)} %get-tuple-element.15), kind=kOutput, calls=%fused_computation.26 | convolution fusion | flops 402710528 | bytes 4194304 | tf_op jit(solution)/shard_map/ckm,jm->ckj/dot_general | solution.py:42
  79.8 3.7 %fusion.14 = f32[128,64,64]{0,2,1:T(8,128)S(1)} fusion(f32[128,64,64]{0,1,2:T(8,128)S(1)} %get-tuple-element.15), kind=kOutput, calls=%fused_computation.24 | convolution fusion | flops 402710528 | bytes 4194304 | tf_op jit(solution)/shard_map/ckm,jm->ckj/dot_general | solution.py:42
  83.5 3.3 %fusion.22 = f32[128,64,64]{0,2,1:T(8,128)S(1)} fusion(f32[128,64,64]{0,2,1:T(8,128)S(1)} %fusion.16, f32[128,64,64]{0,1,2:T(8,128)S(1)} %get-tuple-element.14), kind=kOutput, calls=%fused_computation.32 | convolution fusion | flops 403234816 | bytes 6291456 | tf_op jit(solution)/shard_map/ckm,jm->ckj/dot_general | solution.py:42
  86.8 4.0 %multiply_add_fusion.1 = (f32[128,64,64]{0,2,1:T(8,128)S(1)}, f32[128,64,64]{0,2,1:T(8,128)S(1)}) fusion(f32[128,64,64]{0,2,1:T(8,128)S(1)} %copy-done, f32[128,64,64]{0,2,1:T(8,128)S(1)} %fusion.22, f32[128,64,64]{0,2,1:T(8,128)S(1)} %fusion.31, f32[128,64,64]{0,2,1:T(8,128)S(1)} %fusion.14, f32[128,64,64]{0,1,2:T(8,128)S(1)} %get-tuple-element.14), kind=kOutput, calls=%fused_computation.12 | convolution fusion | flops 406380544 | bytes 14680064 | tf_op jit(solution)/shard_map/ckm,jm->ckj/dot_general | solution.py:42
  90.8 2.2 %fusion.65 = f32[128,64,64]{0,2,1:T(8,128)S(1)} fusion(f32[128,64,64]{0,2,1:T(8,128)S(1)} %get-tuple-element.9), kind=kOutput, calls=%fused_computation.79 | convolution fusion | flops 402710528 | bytes 4194304 | tf_op jit(solution)/shard_map/ckj,mj->ckm/dot_general | solution.py:42
  93.0 2.3 %fusion.61 = f32[128,64,64]{0,2,1:T(8,128)S(1)} fusion(f32[128,64,64]{0,2,1:T(8,128)S(1)} %get-tuple-element.9), kind=kOutput, calls=%fused_computation.75 | convolution fusion | flops 402710528 | bytes 4194304 | tf_op jit(solution)/shard_map/ckj,mj->ckm/dot_general | solution.py:42
  95.3 2.2 %convolution_subtract_fusion = f32[128,64,64]{0,2,1:T(8,128)S(1)} fusion(f32[128,64,64]{0,2,1:T(8,128)S(1)} %fusion.65, f32[128,64,64]{0,2,1:T(8,128)S(1)} %get-tuple-element.8), kind=kOutput, calls=%fused_computation.38 | convolution fusion | flops 403234816 | bytes 6291456 | tf_op jit(solution)/shard_map/ckj,mj->ckm/dot_general | solution.py:42
  97.5 3.2 %multiply_subtract_fusion = (f32[128,64,64]{0,2,1:T(8,128)S(1)}, f32[128,64,64]{0,2,1:T(8,128)S(1)}) fusion(f32[128,64,64]{0,2,1:T(8,128)S(1)} %convolution_subtract_fusion, f32[64,64]{1,0:T(8,128)S(1)} %get-tuple-element.16, f32[64,64]{1,0:T(8,128)S(1)} %get-tuple-element.17, f32[128,64,64]{0,2,1:T(8,128)S(1)} %fusion.61, ...), kind=kOutput, calls=%fused_computation.11 | convolution fusion | flops 406380544 | bytes 10518528 | tf_op jit(solution)/shard_map/ckj,mj->ckm/dot_general | solution.py:42
  100.7 2.5 %fusion.2 = f32[128,64,32]{0,2,1:T(8,128)S(1)} fusion(f32[128,64,64]{0,2,1:T(8,128)S(1)} %get-tuple-element.11), kind=kOutput, calls=%fused_computation.6 | convolution fusion | flops 201355264 | bytes 3145728 | tf_op jit(solution)/shard_map/nk,ckm->cnm/dot_general | solution.py:42
  103.2 2.5 %fusion.40 = f32[128,32,64]{0,1,2:T(8,128)S(1)} fusion(f32[128,64,32]{0,2,1:T(8,128)S(1)} %fusion.2, f32[128,64,64]{0,2,1:T(8,128)S(1)} %get-tuple-element.10), kind=kOutput, calls=%fused_computation.46 | convolution fusion | flops 201879552 | bytes 4194304 | tf_op jit(solution)/shard_map/nk,ckm->cnm/dot_general | solution.py:42
  107.1 13.7 %all_to_all.58 = bf16[128,8,256]{2,0,1:T(8,128)(2,1)S(1)} all-to-all(bf16[128,8,256]{2,0,1:T(8,128)(2,1)S(1)} %add_convert_fusion), channel_id=1, replica_groups=mesh['seq'=8,'chan'=4] {'seq'}, dimensions={1} | all-to-all | bytes 1048576 | tf_op jit(solution)/shard_map/all_to_all | solution.py:139
  121.7 38.7 %all_to_all.59 = bf16[8,512,256]{2,1,0:T(8,128)(2,1)S(1)} all-to-all(bf16[8,512,256]{2,1,0:T(8,128)(2,1)} %bitcast.121), channel_id=1, replica_groups=mesh['seq'=8,'chan'=4] {'seq'}, dimensions={0} | all-to-all | bytes 4194304 | tf_op jit(solution)/shard_map/all_to_all | solution.py:142
  160.4 2.4 %copy.85 = bf16[512,8,256]{0,2,1:T(8,128)(2,1)} copy(bf16[512,8,256]{2,0,1:T(8,128)(2,1)S(1)} %bitcast.118) | data formatting | bytes 4194304 | tf_op jit(solution)/shard_map/all_to_all | solution.py:142
  162.8 7.5 %all-gather.2.cloned.1.call-done = bf16[1024,2048]{1,0:T(8,128)(2,1)} async-done(((bf16[1024,256]{1,0:T(8,128)(2,1)}), bf16[1024,2048]{1,0:T(8,128)(2,1)}) %all-gather.2.cloned.1.call-update) | async-done | bytes 4194320 | tf_op jit(solution)/shard_map/all_gather | solution.py:141
  170.3 5.2 %convolution_bitcast_fusion = f32[512,1024]{0,1:T(8,128)S(1)} fusion(bf16[1024,2048]{1,0:T(8,128)(2,1)} %all-gather.2.cloned.1.call-done, bf16[512,2048]{0,1:T(8,128)(2,1)} %bitcast.122), kind=kOutput, calls=%fused_computation.36 | convolution fusion | flops 2147483648 | bytes 8388608 | tf_op jit(solution)/shard_map/dot_general | solution.py:143
  175.5 1.8 copy.86
  (34 shorter events, 9.1 us)
Async XLA Ops:
  7.2 22.1 %copy-start.2 = (f32[1024,128]{1,0:T(8,128)S(1)}, f32[1024,128]{1,0:T(8,128)}, u32[]{:S(2)}) copy-start(f32[1024,128]{1,0:T(8,128)} %param.9) | copy-start | bytes 1572868
  23.2 9.1 %collective-permute-start = (bf16[1024,128]{1,0:T(8,128)(2,1)S(1)}, bf16[1024,128]{1,0:T(8,128)(2,1)S(1)}, u32[]{:S(2)}, u32[]{:S(2)}) collective-permute-start(bf16[1024,128]{1,0:T(8,128)(2,1)S(1)} %slice.8), channel_id=1, source_target_pairs={{0,4},{4,8},{8,12},{12,16},{16,20},{20,24},{24,28},{1,5},{5,9},{9,... | collective-permute-start | bytes 786440 | tf_op jit(solution)/shard_map/ppermute | solution.py:14
  24.5 25.3 %all-to-all-start.1 = ((bf16[8,128,256]{2,1,0:T(8,128)(2,1)}), bf16[8,128,256]{2,1,0:T(8,128)(2,1)S(1)}, u32[]{:S(2)}, u32[]{:S(2)}) async-start(bf16[8,128,256]{2,1,0:T(8,128)(2,1)} %bitcast.13), calls=%async_computation.1 | async-start | bytes 1048576 | tf_op jit(solution)/shard_map/all_to_all | solution.py:133
  49.8 23.1 %all-to-all-start = ((bf16[8,128,256]{2,1,0:T(8,128)(2,1)}), bf16[8,128,256]{2,1,0:T(8,128)(2,1)S(1)}, u32[]{:S(2)}, u32[]{:S(2)}) async-start(bf16[8,128,256]{2,1,0:T(8,128)(2,1)} %bitcast.2), calls=%async_computation | async-start | bytes 1048576 | tf_op jit(solution)/shard_map/all_to_all | solution.py:132
  54.0 116.3 %all-gather.2.cloned.1.call-start = ((), (), s32[]{:S(2)}) async-start(), calls=%async_computation.4 | async-start | bytes 4718592 | tf_op jit(solution)/shard_map/all_gather | solution.py:141
  83.5 3.3 %copy-start = (f32[128,64,64]{0,2,1:T(8,128)S(1)}, f32[128,64,64]{0,2,1:T(8,128)}, u32[]{:S(2)}) copy-start(f32[128,64,64]{0,2,1:T(8,128)} %fusion.28) | copy-start | bytes 6291460
  106.9 13.9 %copy-start.1 = (bf16[1024,256]{1,0:T(8,128)(2,1)S(1)}, bf16[1024,256]{1,0:T(8,128)(2,1)}, u32[]{:S(2)}) copy-start(bf16[1024,256]{1,0:T(8,128)(2,1)} %param.12) | copy-start | bytes 1572868
Sparse Core Ops, SparseCore 0:
  121.8 48.4 all-gather.1
where the time goes:
time: 188 us; the launch traced here: 184 us
  matrix products  68.7 us (37%)
  blocking collectives  65.9 us (35%)
  between operations  14.6 us (8%)
  local copies, waits for them, and re-layouts  13 us (7%)
  starting transfers between devices  10.3 us (5%)
  waiting for transfers between devices  7.52 us (4%)
  other arithmetic  4.45 us (2%)
    dot_general x14, matrix products, product_einsum(): return jnp.einsum(form, left, right, precision=lax.Precision.HIGHEST)  44.1 us
    all_to_all x1, blocking collectives, shards(): lax.all_to_all(upstream, 'seq', split_axis=0, concat_axis=1, tiled=True)  38.7 us
    all_to_all x1, blocking collectives, shards(): lax.all_to_all(long_whole, 'seq', split_axis=1, concat_axis=0, tiled=True)  13.7 us
    psum x1, blocking collectives, shards(): squares = lax.psum(partial_squares, 'chan')  13.5 us
    conv_general_dilated x1, matrix products, short_conv(): lax.conv_general_dilated(padded[None], kernel, (1,), 'VALID', dimension_n...  12.7 us
    all_gather x1, waiting for transfers between devices, shards(): mixed_whole = lax.all_gather(mixed, 'seq', axis=1, tiled=True)  7.5 us
    dot_general x1, matrix products, shards(): lax.dot_general(owned, mixed_whole, (((1,), (1,)), ((), ())), preferred_e...  5.18 us
    all_to_all x1, starting transfers between devices, shards(): lax.all_to_all(long_filter, 'seq', split_axis=0, concat_axis=1, tiled=True)  4.62 us
  transfers between devices with their start and end apart: 4, of which 1 were waited for; matrix products, arithmetic and copies ran while one was open for 23% of the time, Pallas kernels for 0%

commit v1 on v0

--- a/solution.py
+++ b/solution.py
@@ -136,7 +136,9 @@
     long_whole = (long_conv + bias_slice[:, None] * short_whole.astype(jnp.float32)).astype(
         jnp.bfloat16
     )
-    long_out = lax.all_to_all(long_whole, "seq", split_axis=1, concat_axis=0, tiled=True)
+    pieces = jnp.split(long_whole, lax.axis_size("seq"), axis=1)
+    received = lax.all_to_all(jnp.stack(pieces), "seq", 0, 0)
+    long_out = jnp.concatenate(received, axis=0)
     mixed = (gate_stream.astype(jnp.float32) * long_out.astype(jnp.float32)).astype(jnp.bfloat16)
     mixed_whole = lax.all_gather(mixed, "seq", axis=1, tiled=True)
     owned = lax.all_to_all(upstream, "seq", split_axis=0, concat_axis=1, tiled=True)

time: 188 us -> 191 us (1.016)
  transfers between devices with their start and end apart: 4 -> 4, of which waited for: 1 -> 1; matrix products, arithmetic and copies ran while one was open for 23% -> 22% of each run, Pallas kernels for 0% -> 0%
where the time goes in v1:
time: 191 us; the launch traced here: 187 us
  matrix products  68.7 us (36%)
  blocking collectives  65.9 us (35%)
  between operations  14.6 us (8%)
  local copies, waits for them, and re-layouts  14.5 us (8%)
  starting transfers between devices  10.3 us (5%)
  waiting for transfers between devices  7.52 us (4%)
  other arithmetic  5.44 us (3%)
    dot_general x14, matrix products, product_einsum(): return jnp.einsum(form, left, right, precision=lax.Precision.HIGHEST)  44.1 us
    all_to_all x1, blocking collectives, shards(): lax.all_to_all(upstream, 'seq', split_axis=0, concat_axis=1, tiled=True)  38.7 us
    all_to_all x1, blocking collectives, shards(): received = lax.all_to_all(jnp.stack(pieces), 'seq', 0, 0)  13.7 us
    psum x1, blocking collectives, shards(): squares = lax.psum(partial_squares, 'chan')  13.5 us
    conv_general_dilated x1, matrix products, short_conv(): lax.conv_general_dilated(padded[None], kernel, (1,), 'VALID', dimension_n...  12.7 us
    all_gather x1, waiting for transfers between devices, shards(): mixed_whole = lax.all_gather(mixed, 'seq', axis=1, tiled=True)  7.5 us
    dot_general x1, matrix products, shards(): lax.dot_general(owned, mixed_whole, (((1,), (1,)), ((), ())), preferred_e...  5.18 us
    all_to_all x1, starting transfers between devices, shards(): lax.all_to_all(long_filter, 'seq', split_axis=0, concat_axis=1, tiled=True)  4.62 us
  transfers between devices with their start and end apart: 4, of which 1 were waited for; matrix products, arithmetic and copies ran while one was open for 22% of the time, Pallas kernels for 0%

profile of v1, /device:TPU:0, one launch (start us, length us, event | category | flops | bytes accessed | tf_op | source)
XLA Modules:
  0.0 187.0 jit_solution(1553224910816575011)
XLA Ops:
  7.2 1.3 fusion.43
  8.4 13.5 %psum.7 = f32[256]{0:T(256)S(1)} all-reduce(f32[256]{0:T(256)S(1)} %fusion.43), channel_id=1, replica_groups=mesh['seq'=8,'chan'=4] {'chan'}, use_global_device_ids=true, to_apply=%region_1.0 | all-reduce | flops 256 | bytes 2048 | tf_op jit(solution)/shard_map/psum | solution.py:117
  21.9 1.2 fusion.45
  23.2 1.3 collective-permute-start
  24.5 4.6 %all-to-all-start.1 = ((bf16[8,128,256]{2,1,0:T(8,128)(2,1)}), bf16[8,128,256]{2,1,0:T(8,128)(2,1)S(1)}, u32[]{:S(2)}, u32[]{:S(2)}) async-start(bf16[8,128,256]{2,1,0:T(8,128)(2,1)} %bitcast.13), calls=%async_computation.1 | async-start | bytes 1048576 | tf_op jit(solution)/shard_map/all_to_all | solution.py:133
  32.8 2.2 %copy.55 = bf16[1,1024,383]{1,0,2:T(2,128)(2,1)S(1)} copy(bf16[1,1024,383]{2,1,0:T(8,128)(2,1)S(1)} %maximum_bitcast_fusion) | data formatting | bytes 1568768 | tf_op jit(solution)/shard_map/broadcast_in_dim | solution.py:20
  35.1 12.7 %convolution_convert_fusion = bf16[1,1024,256]{1,0,2:T(2,128)(2,1)S(1)} fusion(bf16[1,1024,383]{1,0,2:T(2,128)(2,1)S(1)} %copy.55, f32[1024,1,128]{0,1,2:T(1,128)} %copy.56), kind=kOutput, calls=%fused_computation.43 | convolution fusion | flops 402915328 | bytes 1832960 | tf_op jit(solution)/shard_map/conv_general_dilated | solution.py:19
  47.8 2.0 %copy.57 = bf16[1,1024,256]{2,1,0:T(8,128)(2,1)} copy(bf16[1,1024,256]{1,0,2:T(2,128)(2,1)S(1)} %convolution_convert_fusion) | data formatting | bytes 1048576 | tf_op jit(solution)/shard_map/convert_element_type | solution.py:130
  49.8 4.2 %all-to-all-start = ((bf16[8,128,256]{2,1,0:T(8,128)(2,1)}), bf16[8,128,256]{2,1,0:T(8,128)(2,1)S(1)}, u32[]{:S(2)}, u32[]{:S(2)}) async-start(bf16[8,128,256]{2,1,0:T(8,128)(2,1)} %bitcast.2), calls=%async_computation | async-start | bytes 1048576 | tf_op jit(solution)/shard_map/all_to_all | solution.py:132
  56.2 1.6 subtract_bitcast_fusion
  57.8 3.3 %fusion.6 = f32[128,64,64]{0,2,1:T(8,128)S(1)} fusion(f32[128,64,64]{0,1,2:T(8,128)S(1)} %get-tuple-element.13), kind=kOutput, calls=%fused_computation.16 | convolution fusion | flops 402710528 | bytes 4194304 | tf_op jit(solution)/shard_map/ckm,jm->ckj/dot_general | solution.py:42
  61.2 3.4 %fusion.31 = f32[128,64,64]{0,2,1:T(8,128)S(1)} fusion(f32[128,64,64]{0,2,1:T(8,128)S(1)} %fusion.6, f32[128,64,64]{0,1,2:T(8,128)S(1)} %get-tuple-element.12), kind=kOutput, calls=%fused_computation.35 | convolution fusion | flops 403234816 | bytes 6291456 | tf_op jit(solution)/shard_map/ckm,jm->ckj/dot_general | solution.py:42
  64.6 3.6 %fusion.8 = f32[128,64,64]{0,2,1:T(8,128)S(1)} fusion(f32[128,64,64]{0,1,2:T(8,128)S(1)} %get-tuple-element.13), kind=kOutput, calls=%fused_computation.18 | convolution fusion | flops 402710528 | bytes 4194304 | tf_op jit(solution)/shard_map/ckm,jm->ckj/dot_general | solution.py:42
  68.1 4.7 %fusion.28 = f32[128,64,64]{0,2,1:T(8,128)} fusion(f32[128,64,64]{0,2,1:T(8,128)S(1)} %fusion.8, f32[128,64,64]{0,1,2:T(8,128)S(1)} %get-tuple-element.12), kind=kOutput, calls=%fused_computation.34 | convolution fusion | flops 403234816 | bytes 6291456 | tf_op jit(solution)/shard_map/ckm,jm->ckj/dot_general | solution.py:42
  74.9 1.6 fusion
  76.5 3.3 %fusion.16 = f32[128,64,64]{0,2,1:T(8,128)S(1)} fusion(f32[128,64,64]{0,1,2:T(8,128)S(1)} %get-tuple-element.15), kind=kOutput, calls=%fused_computation.26 | convolution fusion | flops 402710528 | bytes 4194304 | tf_op jit(solution)/shard_map/ckm,jm->ckj/dot_general | solution.py:42
  79.8 3.7 %fusion.14 = f32[128,64,64]{0,2,1:T(8,128)S(1)} fusion(f32[128,64,64]{0,1,2:T(8,128)S(1)} %get-tuple-element.15), kind=kOutput, calls=%fused_computation.24 | convolution fusion | flops 402710528 | bytes 4194304 | tf_op jit(solution)/shard_map/ckm,jm->ckj/dot_general | solution.py:42
  83.5 3.3 %fusion.22 = f32[128,64,64]{0,2,1:T(8,128)S(1)} fusion(f32[128,64,64]{0,2,1:T(8,128)S(1)} %fusion.16, f32[128,64,64]{0,1,2:T(8,128)S(1)} %get-tuple-element.14), kind=kOutput, calls=%fused_computation.32 | convolution fusion | flops 403234816 | bytes 6291456 | tf_op jit(solution)/shard_map/ckm,jm->ckj/dot_general | solution.py:42
  86.8 4.0 %multiply_add_fusion.1 = (f32[128,64,64]{0,2,1:T(8,128)S(1)}, f32[128,64,64]{0,2,1:T(8,128)S(1)}) fusion(f32[128,64,64]{0,2,1:T(8,128)S(1)} %copy-done, f32[128,64,64]{0,2,1:T(8,128)S(1)} %fusion.22, f32[128,64,64]{0,2,1:T(8,128)S(1)} %fusion.31, f32[128,64,64]{0,2,1:T(8,128)S(1)} %fusion.14, f32[128,64,64]{0,1,2:T(8,128)S(1)} %get-tuple-element.14), kind=kOutput, calls=%fused_computation.12 | convolution fusion | flops 406380544 | bytes 14680064 | tf_op jit(solution)/shard_map/ckm,jm->ckj/dot_general | solution.py:42
  90.8 2.2 %fusion.75 = f32[128,64,64]{0,2,1:T(8,128)S(1)} fusion(f32[128,64,64]{0,2,1:T(8,128)S(1)} %get-tuple-element.9), kind=kOutput, calls=%fused_computation.97 | convolution fusion | flops 402710528 | bytes 4194304 | tf_op jit(solution)/shard_map/ckj,mj->ckm/dot_general | solution.py:42
  93.0 2.3 %fusion.71 = f32[128,64,64]{0,2,1:T(8,128)S(1)} fusion(f32[128,64,64]{0,2,1:T(8,128)S(1)} %get-tuple-element.9), kind=kOutput, calls=%fused_computation.93 | convolution fusion | flops 402710528 | bytes 4194304 | tf_op jit(solution)/shard_map/ckj,mj->ckm/dot_general | solution.py:42
  95.3 2.2 %convolution_subtract_fusion = f32[128,64,64]{0,2,1:T(8,128)S(1)} fusion(f32[128,64,64]{0,2,1:T(8,128)S(1)} %fusion.75, f32[128,64,64]{0,2,1:T(8,128)S(1)} %get-tuple-element.8), kind=kOutput, calls=%fused_computation.38 | convolution fusion | flops 403234816 | bytes 6291456 | tf_op jit(solution)/shard_map/ckj,mj->ckm/dot_general | solution.py:42
  97.5 3.2 %multiply_subtract_fusion = (f32[128,64,64]{0,2,1:T(8,128)S(1)}, f32[128,64,64]{0,2,1:T(8,128)S(1)}) fusion(f32[128,64,64]{0,2,1:T(8,128)S(1)} %convolution_subtract_fusion, f32[64,64]{1,0:T(8,128)S(1)} %get-tuple-element.16, f32[64,64]{1,0:T(8,128)S(1)} %get-tuple-element.17, f32[128,64,64]{0,2,1:T(8,128)S(1)} %fusion.71, ...), kind=kOutput, calls=%fused_computation.11 | convolution fusion | flops 406380544 | bytes 10518528 | tf_op jit(solution)/shard_map/ckj,mj->ckm/dot_general | solution.py:42
  100.7 2.5 %fusion.2 = f32[128,64,32]{0,2,1:T(8,128)S(1)} fusion(f32[128,64,64]{0,2,1:T(8,128)S(1)} %get-tuple-element.11), kind=kOutput, calls=%fused_computation.6 | convolution fusion | flops 201355264 | bytes 3145728 | tf_op jit(solution)/shard_map/nk,ckm->cnm/dot_general | solution.py:42
  103.2 2.5 %fusion.40 = f32[128,32,64]{0,1,2:T(8,128)S(1)} fusion(f32[128,64,32]{0,2,1:T(8,128)S(1)} %fusion.2, f32[128,64,64]{0,2,1:T(8,128)S(1)} %get-tuple-element.10), kind=kOutput, calls=%fused_computation.46 | convolution fusion | flops 201879552 | bytes 4194304 | tf_op jit(solution)/shard_map/nk,ckm->cnm/dot_general | solution.py:42
  107.6 1.5 copy.83
  109.5 13.7 %all_to_all.53 = bf16[8,128,256]{1,2,0:T(8,128)(2,1)S(1)} all-to-all(bf16[8,128,256]{1,2,0:T(8,128)(2,1)S(1)} %fusion.61), channel_id=1, replica_groups=mesh['seq'=8,'chan'=4] {'seq'}, dimensions={0} | all-to-all | bytes 1048576 | tf_op jit(solution)/shard_map/all_to_all | solution.py:140
  124.3 38.7 %all_to_all.54 = bf16[8,512,256]{2,1,0:T(8,128)(2,1)S(1)} all-to-all(bf16[8,512,256]{2,1,0:T(8,128)(2,1)} %bitcast.157), channel_id=1, replica_groups=mesh['seq'=8,'chan'=4] {'seq'}, dimensions={0} | all-to-all | bytes 4194304 | tf_op jit(solution)/shard_map/all_to_all | solution.py:144
  163.0 2.4 %copy.85 = bf16[512,8,256]{0,2,1:T(8,128)(2,1)} copy(bf16[512,8,256]{2,0,1:T(8,128)(2,1)S(1)} %bitcast.155) | data formatting | bytes 4194304 | tf_op jit(solution)/shard_map/all_to_all | solution.py:144
  165.4 7.5 %all-gather.2.cloned.1.call-done = bf16[1024,2048]{1,0:T(8,128)(2,1)} async-done(((bf16[1024,256]{1,0:T(8,128)(2,1)}), bf16[1024,2048]{1,0:T(8,128)(2,1)}) %all-gather.2.cloned.1.call-update) | async-done | bytes 4194320 | tf_op jit(solution)/shard_map/all_gather | solution.py:143
  172.9 5.2 %convolution_bitcast_fusion = f32[512,1024]{0,1:T(8,128)S(1)} fusion(bf16[1024,2048]{1,0:T(8,128)(2,1)} %all-gather.2.cloned.1.call-done, bf16[512,2048]{0,1:T(8,128)(2,1)} %bitcast.158), kind=kOutput, calls=%fused_computation.36 | convolution fusion | flops 2147483648 | bytes 8388608 | tf_op jit(solution)/shard_map/dot_general | solution.py:145
  178.1 1.8 copy.86
  (44 shorter events, 11.1 us)
Async XLA Ops:
  7.2 22.1 %copy-start.1 = (f32[1024,128]{1,0:T(8,128)S(1)}, f32[1024,128]{1,0:T(8,128)}, u32[]{:S(2)}) copy-start(f32[1024,128]{1,0:T(8,128)} %param.9) | copy-start | bytes 1572868
  23.2 9.1 %collective-permute-start = (bf16[1024,128]{1,0:T(8,128)(2,1)S(1)}, bf16[1024,128]{1,0:T(8,128)(2,1)S(1)}, u32[]{:S(2)}, u32[]{:S(2)}) collective-permute-start(bf16[1024,128]{1,0:T(8,128)(2,1)S(1)} %slice.8), channel_id=1, source_target_pairs={{0,4},{4,8},{8,12},{12,16},{16,20},{20,24},{24,28},{1,5},{5,9},{9,... | collective-permute-start | bytes 786440 | tf_op jit(solution)/shard_map/ppermute | solution.py:14
  24.5 25.3 %all-to-all-start.1 = ((bf16[8,128,256]{2,1,0:T(8,128)(2,1)}), bf16[8,128,256]{2,1,0:T(8,128)(2,1)S(1)}, u32[]{:S(2)}, u32[]{:S(2)}) async-start(bf16[8,128,256]{2,1,0:T(8,128)(2,1)} %bitcast.13), calls=%async_computation.1 | async-start | bytes 1048576 | tf_op jit(solution)/shard_map/all_to_all | solution.py:133
  49.8 23.1 %all-to-all-start = ((bf16[8,128,256]{2,1,0:T(8,128)(2,1)}), bf16[8,128,256]{2,1,0:T(8,128)(2,1)S(1)}, u32[]{:S(2)}, u32[]{:S(2)}) async-start(bf16[8,128,256]{2,1,0:T(8,128)(2,1)} %bitcast.2), calls=%async_computation | async-start | bytes 1048576 | tf_op jit(solution)/shard_map/all_to_all | solution.py:132
  54.0 118.9 %all-gather.2.cloned.1.call-start = ((), (), s32[]{:S(2)}) async-start(), calls=%async_computation.4 | async-start | bytes 4718592 | tf_op jit(solution)/shard_map/all_gather | solution.py:143
  83.5 3.3 %copy-start = (f32[128,64,64]{0,2,1:T(8,128)S(1)}, f32[128,64,64]{0,2,1:T(8,128)}, u32[]{:S(2)}) copy-start(f32[128,64,64]{0,2,1:T(8,128)} %fusion.28) | copy-start | bytes 6291460
  109.3 14.1 %copy-start.2 = (bf16[1024,256]{1,0:T(8,128)(2,1)S(1)}, bf16[1024,256]{1,0:T(8,128)(2,1)}, u32[]{:S(2)}) copy-start(bf16[1024,256]{1,0:T(8,128)(2,1)} %param.12) | copy-start | bytes 1572868
Sparse Core Ops, SparseCore 0:
  124.4 48.4 all-gather.1
